TPU v7x, 256 devices: a whole 4x4x8 slice. The times are simulated.
256 devices in a mesh: section: 4 (over x), dp: 64 (over z, y, core).
Axes of the slice: x: 4, y: 4, z: 8, core: 2. Of those that a mesh axis runs over, the one named last changes fastest.
Arguments:
- out_grad: bfloat16 [8192, 5120], P('dp', 'section'), may hold values from -0.26367188 to 0.26367188
- pre_act: bfloat16 [4, 8192, 27648], P('section', 'dp'), may hold values from -6 to 6
- down_a: bfloat16 [4, 27648, 32], P('section'), may hold values from -1 to 1
- down_b: bfloat16 [4, 32, 5120], P('section'), may hold values from -0.078125 to 0.078125
- up_a: bfloat16 [4, 5120, 32], P('section'), may hold values from -1 to 1
- up_b: bfloat16 [4, 27648, 32], P('section'), may hold values from -0.0390625 to 0.0390625
- master: float32 [4, 4, 6912, 32], P('section', None, 'dp'), may hold values from -1 to 1
- moment: float32 [4, 4, 6912, 32], P('section', None, 'dp'), may hold values from -3 to 3
- second: float32 [4, 4, 6912, 32], P('section', None, 'dp'), may hold values from 0.2 to 4
Outputs:
- new_weight: bfloat16 [4, 27648, 32], P('section')
- new_master: float32 [4, 4, 6912, 32], P('section', None, 'dp')
- new_moment: float32 [4, 4, 6912, 32], P('section', None, 'dp')
- new_second: float32 [4, 4, 6912, 32], P('section', None, 'dp')
All inputs are finite; a program needn't handle non-finite values.
Results may differ from a plain program's by a relative error of at most 0.014.
Values may be sent and summed in bfloat16 or wider, within the bound.
No kernel may reach another device: no remote copies, remote signals or barrier semaphores. Data moves between devices by JAX's collectives and lax.ppermute only.
A program may use at most 128 MiB of HBM per device.

v0:
```python
import jax
import jax.numpy as jnp
from jax import lax
from jax.sharding import PartitionSpec as P

BUCKETS = 4
STEP = 20
BETA_ONE = 0.8
BETA_TWO = 0.95
LEARN_RATE = 0.02
DECAY_RATE = 0.1
EPSILON = 1e-08


def shifted(value, axis, steps):
    count = lax.axis_size(axis)
    initial, last = (max(0, -steps), min(count, count - steps))
    return lax.ppermute(value, axis, [(source, source + steps) for source in range(initial, last)])


def slope_of(values):
    sigm = jax.nn.sigmoid(values)
    return sigm * (1.0 + values * (1.0 - sigm))


def adamw(gradient, weights, first, seconds):
    first_new = BETA_ONE * first + (1.0 - BETA_ONE) * gradient
    second_new = BETA_TWO * seconds + (1.0 - BETA_TWO) * gradient * gradient
    first_hat = first_new / (1.0 - BETA_ONE**STEP)
    second_hat = second_new / (1.0 - BETA_TWO**STEP)
    weights_new = weights - LEARN_RATE * (
        first_hat / (jnp.sqrt(second_hat) + EPSILON) + DECAY_RATE * weights
    )
    return (weights_new, first_new, second_new)


def per_device(out_grad, pre_act, down_a, down_b, up_a, up_b, master, moment, second):
    top_grad = lax.all_gather(out_grad, "section", axis=1, tiled=True)
    section_pos = lax.axis_index("section")
    section_count = lax.axis_size("section")
    inputs = pre_act[0].astype(jnp.float32)
    hidden = jax.nn.silu(inputs).astype(jnp.bfloat16)
    slopes = slope_of(inputs)
    factor_a = down_a[0]
    factor_b = down_b[0]
    entry_a = up_a[0]
    entry_b = up_b[0]
    contract_last = (((1,), (1,)), ((), ()))

    def project_low(incoming):
        return lax.dot_general(
            incoming, factor_b, contract_last, preferred_element_type=jnp.float32
        ).astype(jnp.bfloat16)

    current = top_grad
    own_grad = jnp.zeros_like(top_grad)
    for step_index in range(section_count):
        active = section_count - 1 - step_index
        own_grad = jnp.where(section_pos == active, current, own_grad)
        if step_index < section_count - 1:
            low = project_low(current)
            upstream = lax.dot_general(
                low, factor_a, contract_last, preferred_element_type=jnp.float32
            )
            delta = (upstream * slopes).astype(jnp.bfloat16)
            back_low = jnp.dot(delta, entry_b, preferred_element_type=jnp.float32).astype(
                jnp.bfloat16
            )
            carried = lax.dot_general(
                back_low, entry_a, contract_last, preferred_element_type=jnp.float32
            )
            emitted = (current.astype(jnp.float32) + carried).astype(jnp.bfloat16)
            current = shifted(emitted, "section", -1)
    own_low = project_low(own_grad)
    rows_owned = master.shape[2]
    bucket_rows = rows_owned * lax.axis_size("dp")
    contract_first = (((0,), (0,)), ((), ()))
    masters_list = []
    moments_list = []
    seconds_list = []
    pieces = []
    for bucket in range(BUCKETS):
        offset = bucket * bucket_rows

        def bucket_term(start, count, offset=offset):
            columns = lax.dynamic_slice_in_dim(hidden, offset, count, 1)
            return lax.dot_general(
                columns, own_low, contract_first, preferred_element_type=jnp.float32
            )

        shard_grad = lax.psum_scatter(
            bucket_term(jnp.int32(0), rows_owned * lax.axis_size("dp")),
            "dp",
            scatter_dimension=0,
            tiled=True,
        )
        weights_new, first_new, second_new = adamw(
            shard_grad, master[0, bucket], moment[0, bucket], second[0, bucket]
        )
        masters_list.append(weights_new)
        moments_list.append(first_new)
        seconds_list.append(second_new)
        pieces.append(lax.all_gather(weights_new.astype(jnp.bfloat16), "dp", axis=0, tiled=True))
    weights_new = jnp.stack(masters_list)
    first_new = jnp.stack(moments_list)
    second_new = jnp.stack(seconds_list)
    weight_rows = jnp.concatenate(pieces, axis=0)
    return (weight_rows[None], weights_new[None], first_new[None], second_new[None])


def solution(mesh):
    return jax.shard_map(
        per_device,
        mesh=mesh,
        in_specs=(
            P("dp", "section"),
            P("section", "dp", None),
            P("section", None, None),
            P("section", None, None),
            P("section", None, None),
            P("section", None, None),
            P("section", None, "dp", None),
            P("section", None, "dp", None),
            P("section", None, "dp", None),
        ),
        out_specs=(
            P("section", None, None),
            P("section", None, "dp", None),
            P("section", None, "dp", None),
            P("section", None, "dp", None),
        ),
        check_vma=False,
    )
```

profile of v0, /device:TPU:1, one launch (start us, length us, event | category | flops | bytes accessed | tf_op | source)
XLA Modules:
  0.0 589.1 jit_solution(13049837904330362056)
XLA Ops:
  7.2 0.0 all-gather.6.cloned.1.call-start
  7.2 0.7 all-gather.6.cloned.1.call-update
  7.9 0.0 all-reduce.7.cloned.1.call-start
  8.0 31.9 %all-gather.6.cloned.1.call-done = bf16[128,5120]{1,0:T(8,128)(2,1)} async-done(((bf16[128,1280]{1,0:T(8,128)(2,1)}), bf16[128,5120]{1,0:T(8,128)(2,1)}) %all-gather.6.cloned.1.call-update) | async-done | bytes 1310736 | tf_op jit(solution)/shard_map/all_gather | solution.py:38
  39.9 1.9 convolution_convert_fusion.2
  41.8 0.0 copy-done
  41.8 10.0 %fusion.42 = bf16[128,32]{0,1:T(8,128)(2,1)S(1)} fusion(bf16[1,27648,32]{1,2,0:T(8,128)(2,1)S(1)} %copy-done, bf16[128,32]{0,1:T(8,128)(2,1)S(1)} %convolution_convert_fusion.2, bf16[1,27648,32]{1,2,0:T(8,128)(2,1)} %param.11, bf16[1,128,27648]{2,1,0:T(8,128)(2,1)} %param.10), kind=kOutput, calls=%fused_computation.50 | convolution fusion | flops 488378368 | bytes 10633216 | tf_op jit(solution)/shard_map/dot_general | solution.py:66
  51.8 0.1 copy-done.2
  51.9 1.5 fusion.9
  53.4 1.6 collective-permute-start
  55.0 28.7 %collective-permute-done = bf16[128,5120]{1,0:T(8,128)(2,1)S(1)} collective-permute-done((bf16[128,5120]{1,0:T(8,128)(2,1)S(1)}, bf16[128,5120]{1,0:T(8,128)(2,1)S(1)}, u32[]{:S(2)}, u32[]{:S(2)}) %collective-permute-start) | collective-permute-done | bytes 1310752 | tf_op jit(solution)/shard_map/ppermute | solution.py:18
  83.7 1.1 copy-done.3
  84.8 0.5 convolution_convert_fusion.1
  85.3 9.9 %fusion.47 = bf16[128,32]{0,1:T(8,128)(2,1)S(1)} fusion(bf16[1,27648,32]{1,2,0:T(8,128)(2,1)S(1)} %copy-done, bf16[128,32]{0,1:T(8,128)(2,1)S(1)} %convolution_convert_fusion.1, bf16[1,27648,32]{1,2,0:T(8,128)(2,1)} %param.11, bf16[1,128,27648]{2,1,0:T(8,128)(2,1)} %param.10), kind=kOutput, calls=%fused_computation.51 | convolution fusion | flops 488378368 | bytes 10633216 | tf_op jit(solution)/shard_map/dot_general | solution.py:66
  95.2 2.0 add_convert_fusion.1
  97.2 1.8 collective-permute-start.1
  99.1 28.4 %collective-permute-done.1 = bf16[128,5120]{1,0:T(8,128)(2,1)S(1)} collective-permute-done((bf16[128,5120]{1,0:T(8,128)(2,1)S(1)}, bf16[128,5120]{1,0:T(8,128)(2,1)S(1)}, u32[]{:S(2)}, u32[]{:S(2)}) %collective-permute-start.1) | collective-permute-done | bytes 1310752 | tf_op jit(solution)/shard_map/ppermute | solution.py:18
  127.5 1.1 copy-done.4
  128.6 0.5 convolution_convert_fusion
  129.1 9.9 %fusion.52 = bf16[128,32]{0,1:T(8,128)(2,1)S(1)} fusion(bf16[1,27648,32]{1,2,0:T(8,128)(2,1)S(1)} %copy-done, bf16[128,32]{0,1:T(8,128)(2,1)S(1)} %convolution_convert_fusion, bf16[1,27648,32]{1,2,0:T(8,128)(2,1)} %param.11, bf16[1,128,27648]{2,1,0:T(8,128)(2,1)} %param.10), kind=kOutput, calls=%fused_computation.52 | convolution fusion | flops 488378368 | bytes 10633216 | tf_op jit(solution)/shard_map/dot_general | solution.py:66
  139.0 3.1 add_convert_fusion
  142.1 1.5 collective-permute-start.2
  143.6 9.6 %fusion.6 = bf16[128,27648]{1,0:T(8,128)(2,1)} fusion(bf16[1,128,27648]{2,1,0:T(8,128)(2,1)} %param.10), kind=kLoop, calls=%fused_computation.12 | loop fusion | flops 21233664 | bytes 14155776 | tf_op jit(solution)/shard_map/convert_element_type | solution.py:42
  153.2 18.8 %collective-permute-done.2 = bf16[128,5120]{1,0:T(8,128)(2,1)} collective-permute-done((bf16[128,5120]{1,0:T(8,128)(2,1)}, bf16[128,5120]{1,0:T(8,128)(2,1)}, u32[]{:S(2)}, u32[]{:S(2)}) %collective-permute-start.2) | collective-permute-done | bytes 1310752 | tf_op jit(solution)/shard_map/ppermute | solution.py:18
  172.0 1.8 fusion.39
  173.8 1.3 fusion.13
  175.1 1.3 fusion.15
  176.4 1.3 fusion.17
  177.8 1.3 fusion.19
  179.1 0.6 dynamic-slice
  180.3 194.1 %all-reduce.7.cloned.1.call-done = (f32[6912,32]{0,1:T(8,128)}, f32[6912,32]{0,1:T(8,128)}, f32[6912,32]{0,1:T(8,128)}, f32[6912,32]{0,1:T(8,128)}) async-done(((f32[6912,32]{0,1:T(8,128)}, f32[6912,32]{0,1:T(8,128)}, f32[6912,32]{0,1:T(8,128)}, f32[6912,32]{0,1:T(8,128)}), (f32[6912,32]{0,1:T(8,128)}, f32[6912,32]{0,1:T(8,128)}, f32[6912,32]{0,1:T(8,128)}, ...) | async-done | bytes 3538960
  374.5 0.9 convert_bitcast_fusion.3
  375.3 0.9 convert_bitcast_fusion
  376.2 50.7 %all-gather.1 = bf16[64,108,32]{1,2,0:T(8,128)(2,1)S(1)} all-gather(bf16[1,108,32]{1,2,0:T(8,128)(2,1)S(1)} %get-tuple-element.30), channel_id=1, replica_groups=mesh['section'=4,'dp'=64] {'dp'}, dimensions={0}, use_global_device_ids=true | all-gather | bytes 449280 | tf_op jit(solution)/shard_map/all_gather | solution.py:103
  427.0 0.2 copy.18
  427.2 0.8 reshape.30
  427.9 48.7 %all-gather.2 = bf16[64,108,32]{1,2,0:T(8,128)(2,1)S(1)} all-gather(bf16[1,108,32]{1,2,0:T(8,128)(2,1)S(1)} %get-tuple-element.26), channel_id=1, replica_groups=mesh['section'=4,'dp'=64] {'dp'}, dimensions={0}, use_global_device_ids=true | all-gather | bytes 449280 | tf_op jit(solution)/shard_map/all_gather | solution.py:103
  476.7 0.2 copy.19
  476.9 0.8 reshape.32
  477.7 48.6 %all-gather.3 = bf16[64,108,32]{1,2,0:T(8,128)(2,1)S(1)} all-gather(bf16[1,108,32]{1,2,0:T(8,128)(2,1)S(1)} %get-tuple-element.14), channel_id=1, replica_groups=mesh['section'=4,'dp'=64] {'dp'}, dimensions={0}, use_global_device_ids=true | all-gather | bytes 449280 | tf_op jit(solution)/shard_map/all_gather | solution.py:103
  526.3 0.2 copy.20
  526.5 1.5 reshape.34
  528.0 48.5 %all-gather = bf16[64,108,32]{1,2,0:T(8,128)(2,1)S(1)} all-gather(bf16[1,108,32]{1,2,0:T(8,128)(2,1)S(1)} %get-tuple-element.8), channel_id=1, replica_groups=mesh['section'=4,'dp'=64] {'dp'}, dimensions={0}, use_global_device_ids=true | all-gather | bytes 449280 | tf_op jit(solution)/shard_map/all_gather | solution.py:103
  576.5 0.2 copy.17
  576.7 1.5 reshape.28
  578.2 0.6 maximum_bitcast_fusion.1
  578.9 2.5 maximum_bitcast_fusion
  581.4 0.7 maximum_bitcast_fusion.2
  (17 shorter events, 0.1 us)
Async XLA Ops:
  7.2 34.6 %copy-start = (bf16[1,27648,32]{1,2,0:T(8,128)(2,1)S(1)}, bf16[1,27648,32]{1,2,0:T(8,128)(2,1)}, u32[]{:S(2)}) copy-start(bf16[1,27648,32]{1,2,0:T(8,128)(2,1)} %param.14) | copy-start | bytes 5308420
  7.2 32.7 %all-gather.6.cloned.1.call-start = ((), (), s32[]{:S(2)}) async-start(), calls=%async_computation | async-start | bytes 1638400 | tf_op jit(solution)/shard_map/all_gather | solution.py:38
  7.9 366.5 %all-reduce.7.cloned.1.call-start = ((), (), s32[]{:S(2)}) async-start(), calls=%async_computation.1 | async-start | bytes 7077888
  41.8 10.0 %copy-start.2 = (bf16[128,5120]{1,0:T(8,128)(2,1)S(1)}, bf16[128,5120]{1,0:T(8,128)(2,1)}, u32[]{:S(2)}) copy-start(bf16[128,5120]{1,0:T(8,128)(2,1)} %all-gather.6.cloned.1.call-done) | copy-start | bytes 3932164
  51.9 32.9 %copy-start.5 = (bf16[1,32,5120]{2,1,0:T(8,128)(2,1)S(1)}, bf16[1,32,5120]{2,1,0:T(8,128)(2,1)}, u32[]{:S(2)}) copy-start(bf16[1,32,5120]{2,1,0:T(8,128)(2,1)} %param.12) | copy-start | bytes 983044
  53.4 30.3 %collective-permute-start = (bf16[128,5120]{1,0:T(8,128)(2,1)S(1)}, bf16[128,5120]{1,0:T(8,128)(2,1)S(1)}, u32[]{:S(2)}, u32[]{:S(2)}) collective-permute-start(bf16[128,5120]{1,0:T(8,128)(2,1)S(1)} %fusion.9), channel_id=1, source_target_pairs={{64,0},{128,64},{192,128},{65,1},{129,65},{193,129},{66,2},{130,66... | collective-permute-start | bytes 3932168 | tf_op jit(solution)/shard_map/ppermute | solution.py:18
  83.7 1.1 copy-start.3
  97.2 30.2 %collective-permute-start.1 = (bf16[128,5120]{1,0:T(8,128)(2,1)S(1)}, bf16[128,5120]{1,0:T(8,128)(2,1)S(1)}, u32[]{:S(2)}, u32[]{:S(2)}) collective-permute-start(bf16[128,5120]{1,0:T(8,128)(2,1)S(1)} %add_convert_fusion.1), channel_id=1, source_target_pairs={{64,0},{128,64},{192,128},{65,1},{129,65},{193,129},{66,2},{130,66... | collective-permute-start | bytes 3932168 | tf_op jit(solution)/shard_map/ppermute | solution.py:18
  127.5 1.1 copy-start.4
  142.1 29.9 %collective-permute-start.2 = (bf16[128,5120]{1,0:T(8,128)(2,1)}, bf16[128,5120]{1,0:T(8,128)(2,1)}, u32[]{:S(2)}, u32[]{:S(2)}) collective-permute-start(bf16[128,5120]{1,0:T(8,128)(2,1)} %add_convert_fusion), channel_id=1, source_target_pairs={{64,0},{128,64},{192,128},{65,1},{129,65},{193,129},{66,2},{130,66... | collective-permute-start | bytes 3932168 | tf_op jit(solution)/shard_map/ppermute | solution.py:18
  153.2 20.6 %copy-start.1 = (bf16[128,27648]{1,0:T(8,128)(2,1)S(1)}, bf16[128,27648]{1,0:T(8,128)(2,1)}, u32[]{:S(2)}) copy-start(bf16[128,27648]{1,0:T(8,128)(2,1)} %fusion.6) | copy-start | bytes 21233668
  177.8 1.3 copy-start.9
  177.8 196.7 %copy-start.6 = (f32[1,4,108,32]{2,3,1,0:T(8,128)S(1)}, f32[1,4,108,32]{2,3,1,0:T(8,128)}, u32[]{:S(2)}) copy-start(f32[1,4,108,32]{2,3,1,0:T(8,128)} %param.17) | copy-start | bytes 165892
  177.8 196.7 %copy-start.7 = (f32[1,4,108,32]{2,3,1,0:T(8,128)S(1)}, f32[1,4,108,32]{2,3,1,0:T(8,128)}, u32[]{:S(2)}) copy-start(f32[1,4,108,32]{2,3,1,0:T(8,128)} %param.16) | copy-start | bytes 165892
  177.8 196.7 %copy-start.8 = (f32[1,4,108,32]{2,3,1,0:T(8,128)S(1)}, f32[1,4,108,32]{2,3,1,0:T(8,128)}, u32[]{:S(2)}) copy-start(f32[1,4,108,32]{2,3,1,0:T(8,128)} %param.15) | copy-start | bytes 165892
Sparse Core Ops, SparseCore 0:
  9.8 30.0 all-gather.5
  179.2 195.1 all-reduce.6
where the time goes:
time: 595 us; the launch traced here: 589 us
  waiting for transfers between devices  303 us (51%)
  blocking collectives  197 us (33%)
  matrix products  46.4 us (8%)
  other arithmetic  15.2 us (3%)
  between operations  15.1 us (3%)
  local copies, waits for them, and re-layouts  8.34 us (1%)
    all_gather x4, blocking collectives, per_device(): lax.all_gather(weights_new.astype(jnp.bfloat16), 'dp', axis=0, tiled=True)  197 us
    unnamed x3, waiting for transfers between devices  195 us
    ppermute x3, waiting for transfers between devices, shifted(): lax.ppermute(value, axis, [(source, source + steps) for source in range(i...  75.9 us
    all_gather x1, waiting for transfers between devices, per_device(): top_grad = lax.all_gather(out_grad, 'section', axis=1, tiled=True)  31.9 us
    dot_general x3, matrix products, per_device(): jnp.dot(delta, entry_b, preferred_element_type=jnp.float32)  29.8 us
  transfers between devices with their start and end apart: 5, of which 5 were waited for; matrix products, arithmetic and copies ran while one was open for 2% of the time, Pallas kernels for 0%

commit v1 on v0

--- a/solution.py
+++ b/solution.py
@@ -10,6 +10,24 @@
 LEARN_RATE = 0.02
 DECAY_RATE = 0.1
 EPSILON = 1e-08
+
+
+def collect(value, axis, dim):
+    ways, here, step = (lax.axis_size(axis), lax.axis_index(axis), value.shape[dim])
+    dims = [n * ways if d == dim else n for d, n in enumerate(value.shape)]
+    full = lax.dynamic_update_slice_in_dim(
+        jnp.zeros(dims, value.dtype), value, here * step, axis=dim
+    )
+    going_up = going_down = value
+    for far in range(1, ways // 2 + 1):
+        going_up = lax.ppermute(going_up, axis, [(d, (d + 1) % ways) for d in range(ways)])
+        full = lax.dynamic_update_slice_in_dim(full, going_up, (here - far) % ways * step, axis=dim)
+        if 2 * far < ways:
+            going_down = lax.ppermute(going_down, axis, [(d, (d - 1) % ways) for d in range(ways)])
+            full = lax.dynamic_update_slice_in_dim(
+                full, going_down, (here + far) % ways * step, axis=dim
+            )
+    return full
 
 
 def shifted(value, axis, steps):
@@ -35,7 +53,7 @@
 
 
 def per_device(out_grad, pre_act, down_a, down_b, up_a, up_b, master, moment, second):
-    top_grad = lax.all_gather(out_grad, "section", axis=1, tiled=True)
+    top_grad = collect(out_grad, "section", 1)
     section_pos = lax.axis_index("section")
     section_count = lax.axis_size("section")
     inputs = pre_act[0].astype(jnp.float32)

time: 595 us -> 581 us (0.976)
  waiting for transfers between devices: 303 us -> 279 us
    all_gather x1 -> x0, waiting for transfers between devices: 31.9 us -> none  [per_device(): top_grad = lax.all_gather(out_grad, 'section', axis=1, tiled=True)]
    ppermute x0 -> x3, waiting for transfers between devices: none -> 8.86 us  [the longest x2 8.85 us: collect(): lax.ppermute(going_up, axis, [(d, (d + 1) % ways) for d in range(ways)])]
    unnamed x3 -> x2, waiting for transfers between devices: 195 us -> 198 us
  transfers between devices with their start and end apart: 5 -> 7, of which waited for: 5 -> 6; matrix products, arithmetic and copies ran while one was open for 2% -> 2% of each run, Pallas kernels for 0% -> 0%
where the time goes in v1:
time: 581 us; the launch traced here: 573 us
  waiting for transfers between devices  279 us (48%)
  blocking collectives  197 us (34%)
  matrix products  44.9 us (8%)
  other arithmetic  15.2 us (3%)
  between operations  15.1 us (3%)
  local copies, waits for them, and re-layouts  12.1 us (2%)
  starting transfers between devices  10.2 us (2%)
    unnamed x2, waiting for transfers between devices  198 us
    all_gather x4, blocking collectives, per_device(): lax.all_gather(weights_new.astype(jnp.bfloat16), 'dp', axis=0, tiled=True)  197 us
    ppermute x3, waiting for transfers between devices, shifted(): lax.ppermute(value, axis, [(source, source + steps) for source in range(i...  72 us
    dot_general x3, matrix products, per_device(): jnp.dot(delta, entry_b, preferred_element_type=jnp.float32)  29.7 us
  transfers between devices with their start and end apart: 7, of which 6 were waited for; matrix products, arithmetic and copies ran while one was open for 2% of the time, Pallas kernels for 0%

profile of v1, /device:TPU:1, one launch (start us, length us, event | category | flops | bytes accessed | tf_op | source)
XLA Modules:
  0.0 573.3 jit_solution(13333307377721276658)
XLA Ops:
  7.2 2.1 collective-permute-start
  9.3 1.4 collective-permute-start.1
  10.8 1.0 constant_dynamic-update-slice_fusion.3
  11.9 4.2 collective-permute-done
  16.1 1.9 collective-permute-start.2
  17.9 1.0 constant_dynamic-update-slice_fusion.2
  19.0 1.0 constant_dynamic-update-slice_fusion.1
  20.0 4.7 collective-permute-done.2
  24.7 0.5 convolution_convert_fusion.2
  25.3 9.9 %fusion.41 = bf16[128,32]{0,1:T(8,128)(2,1)S(1)} fusion(bf16[1,27648,32]{1,2,0:T(8,128)(2,1)S(1)} %copy-done, bf16[128,32]{0,1:T(8,128)(2,1)S(1)} %convolution_convert_fusion.2, bf16[1,27648,32]{1,2,0:T(8,128)(2,1)} %param.11, bf16[1,128,27648]{2,1,0:T(8,128)(2,1)} %param.10), kind=kOutput, calls=%fused_computation.49 | convolution fusion | flops 488378368 | bytes 10633216 | tf_op jit(solution)/shard_map/dot_general | solution.py:84
  35.2 1.6 add_convert_fusion.2
  36.7 1.6 collective-permute-start.3
  38.3 26.9 %collective-permute-done.3 = bf16[128,5120]{1,0:T(8,128)(2,1)S(1)} collective-permute-done((bf16[128,5120]{1,0:T(8,128)(2,1)S(1)}, bf16[128,5120]{1,0:T(8,128)(2,1)S(1)}, u32[]{:S(2)}, u32[]{:S(2)}) %collective-permute-start.3) | collective-permute-done | bytes 1310752 | tf_op jit(solution)/shard_map/ppermute | solution.py:36
  65.2 1.1 copy-done.2
  66.3 0.5 convolution_convert_fusion.1
  66.8 9.9 %fusion.46 = bf16[128,32]{0,1:T(8,128)(2,1)S(1)} fusion(bf16[1,27648,32]{1,2,0:T(8,128)(2,1)S(1)} %copy-done, bf16[128,32]{0,1:T(8,128)(2,1)S(1)} %convolution_convert_fusion.1, bf16[1,27648,32]{1,2,0:T(8,128)(2,1)} %param.11, bf16[1,128,27648]{2,1,0:T(8,128)(2,1)} %param.10), kind=kOutput, calls=%fused_computation.50 | convolution fusion | flops 488378368 | bytes 10633216 | tf_op jit(solution)/shard_map/dot_general | solution.py:84
  76.7 2.0 add_convert_fusion.1
  78.7 1.8 collective-permute-start.4
  80.5 27.7 %collective-permute-done.4 = bf16[128,5120]{1,0:T(8,128)(2,1)S(1)} collective-permute-done((bf16[128,5120]{1,0:T(8,128)(2,1)S(1)}, bf16[128,5120]{1,0:T(8,128)(2,1)S(1)}, u32[]{:S(2)}, u32[]{:S(2)}) %collective-permute-start.4) | collective-permute-done | bytes 1310752 | tf_op jit(solution)/shard_map/ppermute | solution.py:36
  108.3 1.1 copy-done.3
  109.4 0.5 convolution_convert_fusion
  109.9 9.9 %fusion.51 = bf16[128,32]{0,1:T(8,128)(2,1)S(1)} fusion(bf16[1,27648,32]{1,2,0:T(8,128)(2,1)S(1)} %copy-done, bf16[128,32]{0,1:T(8,128)(2,1)S(1)} %convolution_convert_fusion, bf16[1,27648,32]{1,2,0:T(8,128)(2,1)} %param.11, bf16[1,128,27648]{2,1,0:T(8,128)(2,1)} %param.10), kind=kOutput, calls=%fused_computation.51 | convolution fusion | flops 488378368 | bytes 10633216 | tf_op jit(solution)/shard_map/dot_general | solution.py:84
  119.8 3.1 add_convert_fusion
  122.9 1.5 collective-permute-start.5
  124.3 9.7 %fusion.6 = bf16[128,27648]{1,0:T(8,128)(2,1)} fusion(bf16[1,128,27648]{2,1,0:T(8,128)(2,1)} %param.10), kind=kLoop, calls=%fused_computation.12 | loop fusion | flops 21233664 | bytes 14155776 | tf_op jit(solution)/shard_map/convert_element_type | solution.py:60
  134.0 17.4 %collective-permute-done.5 = bf16[128,5120]{1,0:T(8,128)(2,1)} collective-permute-done((bf16[128,5120]{1,0:T(8,128)(2,1)}, bf16[128,5120]{1,0:T(8,128)(2,1)}, u32[]{:S(2)}, u32[]{:S(2)}) %collective-permute-start.5) | collective-permute-done | bytes 1310752 | tf_op jit(solution)/shard_map/ppermute | solution.py:36
  151.4 1.8 fusion.38
  153.2 1.3 fusion.12
  154.5 1.3 fusion.14
  155.8 1.3 fusion.16
  157.1 1.3 fusion.18
  158.5 0.6 copy-done.8
  159.1 0.6 dynamic-slice
  160.3 198.3 %all-reduce.7.cloned.1.call-done = (f32[6912,32]{0,1:T(8,128)}, f32[6912,32]{0,1:T(8,128)}, f32[6912,32]{0,1:T(8,128)}, f32[6912,32]{0,1:T(8,128)}) async-done(((f32[6912,32]{0,1:T(8,128)}, f32[6912,32]{0,1:T(8,128)}, f32[6912,32]{0,1:T(8,128)}, f32[6912,32]{0,1:T(8,128)}), (f32[6912,32]{0,1:T(8,128)}, f32[6912,32]{0,1:T(8,128)}, f32[6912,32]{0,1:T(8,128)}, ...) | async-done | bytes 3538960
  358.7 0.9 convert_bitcast_fusion.3
  359.5 0.9 convert_bitcast_fusion
  360.4 50.7 %all-gather.1 = bf16[64,108,32]{1,2,0:T(8,128)(2,1)S(1)} all-gather(bf16[1,108,32]{1,2,0:T(8,128)(2,1)S(1)} %get-tuple-element.30), channel_id=1, replica_groups=mesh['section'=4,'dp'=64] {'dp'}, dimensions={0}, use_global_device_ids=true | all-gather | bytes 449280 | tf_op jit(solution)/shard_map/all_gather | solution.py:121
  411.2 0.2 copy.18
  411.4 0.8 reshape.30
  412.2 48.7 %all-gather.2 = bf16[64,108,32]{1,2,0:T(8,128)(2,1)S(1)} all-gather(bf16[1,108,32]{1,2,0:T(8,128)(2,1)S(1)} %get-tuple-element.26), channel_id=1, replica_groups=mesh['section'=4,'dp'=64] {'dp'}, dimensions={0}, use_global_device_ids=true | all-gather | bytes 449280 | tf_op jit(solution)/shard_map/all_gather | solution.py:121
  461.1 0.8 reshape.32
  461.9 48.6 %all-gather.3 = bf16[64,108,32]{1,2,0:T(8,128)(2,1)S(1)} all-gather(bf16[1,108,32]{1,2,0:T(8,128)(2,1)S(1)} %get-tuple-element.14), channel_id=1, replica_groups=mesh['section'=4,'dp'=64] {'dp'}, dimensions={0}, use_global_device_ids=true | all-gather | bytes 449280 | tf_op jit(solution)/shard_map/all_gather | solution.py:121
  510.7 1.5 reshape.34
  512.2 48.5 %all-gather = bf16[64,108,32]{1,2,0:T(8,128)(2,1)S(1)} all-gather(bf16[1,108,32]{1,2,0:T(8,128)(2,1)S(1)} %get-tuple-element.8), channel_id=1, replica_groups=mesh['section'=4,'dp'=64] {'dp'}, dimensions={0}, use_global_device_ids=true | all-gather | bytes 449280 | tf_op jit(solution)/shard_map/all_gather | solution.py:121
  560.9 1.5 reshape.28
  562.4 0.6 maximum_bitcast_fusion.1
  563.1 2.5 maximum_bitcast_fusion
  565.5 0.7 maximum_bitcast_fusion.2
  (23 shorter events, 0.9 us)
Async XLA Ops:
  7.2 18.1 %copy-start = (bf16[1,27648,32]{1,2,0:T(8,128)(2,1)S(1)}, bf16[1,27648,32]{1,2,0:T(8,128)(2,1)}, u32[]{:S(2)}) copy-start(bf16[1,27648,32]{1,2,0:T(8,128)(2,1)} %param.14) | copy-start | bytes 5308420
  7.2 351.5 %all-reduce.7.cloned.1.call-start = ((), (), s32[]{:S(2)}) async-start(), calls=%async_computation | async-start | bytes 7077888
  7.2 8.8 %collective-permute-start = (bf16[128,1280]{1,0:T(8,128)(2,1)}, bf16[128,1280]{1,0:T(8,128)(2,1)}, u32[]{:S(2)}, u32[]{:S(2)}) collective-permute-start(bf16[128,1280]{1,0:T(8,128)(2,1)} %param.9), channel_id=1, source_target_pairs={{0,64},{64,128},{128,192},{192,0},{1,65},{65,129},{129,193},{193,1... | collective-permute-start | bytes 983048 | tf_op jit(solution)/shard_map/ppermute | solution.py:23
  9.3 9.6 %collective-permute-start.1 = (bf16[128,1280]{1,0:T(8,128)(2,1)}, bf16[128,1280]{1,0:T(8,128)(2,1)}, u32[]{:S(2)}, u32[]{:S(2)}) collective-permute-start(bf16[128,1280]{1,0:T(8,128)(2,1)} %param.9), channel_id=1, source_target_pairs={{0,192},{64,0},{128,64},{192,128},{1,193},{65,1},{129,65},{193,129... | collective-permute-start | bytes 983048 | tf_op jit(solution)/shard_map/ppermute | solution.py:26
  10.7 14.0 %copy-start.4 = (bf16[1,32,5120]{2,1,0:T(8,128)(2,1)S(1)}, bf16[1,32,5120]{2,1,0:T(8,128)(2,1)}, u32[]{:S(2)}) copy-start(bf16[1,32,5120]{2,1,0:T(8,128)(2,1)} %param.12) | copy-start | bytes 983044
  16.1 8.6 %collective-permute-start.2 = (bf16[128,1280]{1,0:T(8,128)(2,1)}, bf16[128,1280]{1,0:T(8,128)(2,1)S(1)}, u32[]{:S(2)}, u32[]{:S(2)}) collective-permute-start(bf16[128,1280]{1,0:T(8,128)(2,1)} %collective-permute-done), channel_id=1, source_target_pairs={{0,64},{64,128},{128,192},{192,0},{1,65},{65,129},{129,193},{193,1... | collective-permute-start | bytes 983048 | tf_op jit(solution)/shard_map/ppermute | solution.py:23
  36.7 28.5 %collective-permute-start.3 = (bf16[128,5120]{1,0:T(8,128)(2,1)S(1)}, bf16[128,5120]{1,0:T(8,128)(2,1)S(1)}, u32[]{:S(2)}, u32[]{:S(2)}) collective-permute-start(bf16[128,5120]{1,0:T(8,128)(2,1)S(1)} %add_convert_fusion.2), channel_id=1, source_target_pairs={{64,0},{128,64},{192,128},{65,1},{129,65},{193,129},{66,2},{130,66... | collective-permute-start | bytes 3932168 | tf_op jit(solution)/shard_map/ppermute | solution.py:36
  65.2 1.1 copy-start.2
  78.7 29.6 %collective-permute-start.4 = (bf16[128,5120]{1,0:T(8,128)(2,1)S(1)}, bf16[128,5120]{1,0:T(8,128)(2,1)S(1)}, u32[]{:S(2)}, u32[]{:S(2)}) collective-permute-start(bf16[128,5120]{1,0:T(8,128)(2,1)S(1)} %add_convert_fusion.1), channel_id=1, source_target_pairs={{64,0},{128,64},{192,128},{65,1},{129,65},{193,129},{66,2},{130,66... | collective-permute-start | bytes 3932168 | tf_op jit(solution)/shard_map/ppermute | solution.py:36
  108.3 1.1 copy-start.3
  122.9 28.5 %collective-permute-start.5 = (bf16[128,5120]{1,0:T(8,128)(2,1)}, bf16[128,5120]{1,0:T(8,128)(2,1)}, u32[]{:S(2)}, u32[]{:S(2)}) collective-permute-start(bf16[128,5120]{1,0:T(8,128)(2,1)} %add_convert_fusion), channel_id=1, source_target_pairs={{64,0},{128,64},{192,128},{65,1},{129,65},{193,129},{66,2},{130,66... | collective-permute-start | bytes 3932168 | tf_op jit(solution)/shard_map/ppermute | solution.py:36
  134.0 19.2 %copy-start.1 = (bf16[128,27648]{1,0:T(8,128)(2,1)S(1)}, bf16[128,27648]{1,0:T(8,128)(2,1)}, u32[]{:S(2)}) copy-start(bf16[128,27648]{1,0:T(8,128)(2,1)} %fusion.6) | copy-start | bytes 21233668
  158.4 0.7 copy-start.8
  158.4 200.2 %copy-start.5 = (f32[1,4,108,32]{2,3,1,0:T(8,128)S(1)}, f32[1,4,108,32]{2,3,1,0:T(8,128)}, u32[]{:S(2)}) copy-start(f32[1,4,108,32]{2,3,1,0:T(8,128)} %param.17) | copy-start | bytes 165892
  158.4 200.2 %copy-start.6 = (f32[1,4,108,32]{2,3,1,0:T(8,128)S(1)}, f32[1,4,108,32]{2,3,1,0:T(8,128)}, u32[]{:S(2)}) copy-start(f32[1,4,108,32]{2,3,1,0:T(8,128)} %param.16) | copy-start | bytes 165892
  158.4 200.2 %copy-start.7 = (f32[1,4,108,32]{2,3,1,0:T(8,128)S(1)}, f32[1,4,108,32]{2,3,1,0:T(8,128)}, u32[]{:S(2)}) copy-start(f32[1,4,108,32]{2,3,1,0:T(8,128)} %param.15) | copy-start | bytes 165892
Sparse Core Ops, SparseCore 0:
  158.6 200.0 all-reduce.6
